TPU v7x, 512 devices: a whole 4x4x16 slice. The times are simulated.
512 devices in a mesh: dp: 16 (over x_lo, y, core), vocab: 32 (over z, x_hi).
Axes of the slice: x: 4 (x_hi: 2, x_lo: 2; x = x_hi * 2 + x_lo), y: 4, z: 16, core: 2. Of those that a mesh axis runs over, the one named last changes fastest.
Arguments:
- passage_hidden: bfloat16 [2048, 2048], P('dp'), may hold values from -7 to 7
- passage_lengths: int32 [32], P('dp'), may hold values from 16 to 64, as said below
- query_ids: int32 [32, 16], P('dp'), may hold values from 0 to 131071
- query_lengths: int32 [32], P('dp'), may hold values from 4 to 16, as said below
- positives: int32 [32], replicated, may hold values from 0 to 31, each once
- head: bfloat16 [2048, 131072], P('dp', 'vocab'), may hold values from -0.125 to 0.125
- df_prev: float32 [131072], P('vocab'), may hold values from 1 to 4096
Outputs:
- head_grad: float32 [2048, 131072], P('dp', 'vocab')
- scores: float32 [32, 32], replicated
Inputs may be any that keep to these rules, and one draw needn't show every extreme that they name: `passage_lengths`: some passage fills all 64 slots. `query_lengths`: some query fills all 16 slots. `positives`: each passage is the positive of exactly one query.
All inputs are finite; a program needn't handle non-finite values.
Results may differ from a plain program's by a relative error of at most 0.00064.
Values may be sent and summed in bfloat16 or wider, within the bound.
No kernel may reach another device: no remote copies, remote signals or barrier semaphores. Data moves between devices by JAX's collectives and lax.ppermute only.
A program may use at most 64 MiB of HBM per device.

v0:
```python
import jax
import jax.numpy as jnp
from jax import lax
from jax.sharding import Mesh, PartitionSpec as P

flops_weight = 0.3
DP = ("xl", "y", "c")
VOCAB = ("z", "xh")
PLANE = ("xl", "y", "c", "xh")


def ranking_grad(scores, chosen, query_total):
    columns = scores.shape[1]
    onehot = (jnp.arange(columns, dtype=jnp.int32)[None, :] == chosen[:, None]).astype(jnp.float32)
    own_score = jnp.sum(scores * onehot, axis=1, keepdims=True)
    sigmas = jax.nn.sigmoid(scores - own_score)
    return (sigmas - onehot * jnp.sum(sigmas, axis=1, keepdims=True)) / query_total


def spread(value, axes):
    count = lax.axis_size(axes)
    return lax.all_to_all(
        jnp.broadcast_to(value[None], (count,) + value.shape), axes, 0, 0, tiled=True
    )


def local(passage_hidden, passage_lengths, query_ids, query_lengths, positives, head, df_prev):
    dp_count = lax.axis_size(DP)
    dp_index = lax.axis_index(DP)
    vocab_index = lax.axis_index(VOCAB)
    width_local = head.shape[1]
    column_count = width_local // dp_count
    query_slots = query_ids.shape[1]
    packed = jnp.concatenate([query_ids, query_lengths[:, None], passage_lengths[:, None]], axis=1)
    packed = spread(packed, DP).reshape(-1, query_slots + 2)
    query_tokens = packed[:, :query_slots]
    query_sizes = packed[:, query_slots]
    passage_sizes = packed[:, query_slots + 1]
    head_block = lax.all_to_all(head, DP, split_axis=1, concat_axis=0, tiled=True)
    hidden_all = lax.all_gather(passage_hidden, DP, axis=0, tiled=True)
    passage_count = passage_sizes.shape[0]
    seq_span = hidden_all.shape[0] // passage_count
    logits = jnp.dot(hidden_all, head_block, preferred_element_type=jnp.float32)
    softened = jax.nn.softplus(logits)
    activation = jnp.log1p(softened)
    slope_term = jax.nn.sigmoid(logits) / (1.0 + softened)
    positions = jnp.arange(seq_span, dtype=jnp.int32)
    token_mask = (positions[None, :] < passage_sizes[:, None]).astype(jnp.float32)
    token_weight = token_mask / passage_sizes.astype(jnp.float32)[:, None]
    passage_rep = jnp.sum(
        activation.reshape(passage_count, seq_span, column_count) * token_weight[:, :, None], axis=1
    )
    first_column = dp_index * column_count
    doc_freq = lax.dynamic_slice_in_dim(df_prev, first_column, column_count, 0) + jnp.sum(
        1.0 - jnp.exp(-2.0 * passage_rep), axis=0
    )
    term_weight = jnp.log1p(doc_freq)
    column_ids = (
        vocab_index * width_local + first_column + jnp.arange(column_count, dtype=jnp.int32)
    )
    query_mask = jnp.arange(query_slots, dtype=jnp.int32)[None, :] < query_sizes[:, None]
    matches = (query_tokens[:, :, None] == column_ids[None, None, :]) & query_mask[:, :, None]
    query_bag = jnp.sum(matches.astype(jnp.float32), axis=1)
    partial_scores = jnp.dot(
        query_bag,
        passage_rep.T,
        precision=lax.Precision.HIGHEST,
        preferred_element_type=jnp.float32,
    )
    query_total = positives.shape[0]
    plane_scores = jnp.sum(spread(partial_scores, PLANE), axis=0)
    scores = jnp.sum(spread(plane_scores, "z"), axis=0)
    score_grad = ranking_grad(scores, positives, query_total)
    rep_grad = jnp.dot(
        score_grad.T, query_bag, precision=lax.Precision.HIGHEST, preferred_element_type=jnp.float32
    )
    rep_grad = rep_grad + 2.0 * flops_weight / passage_count * term_weight * jnp.mean(
        passage_rep, axis=0
    )
    logit_grad = (
        (token_weight[:, :, None] * rep_grad[:, None, :]).reshape(logits.shape) * slope_term
    ).astype(jnp.bfloat16)
    grad_block = lax.dot_general(
        hidden_all, logit_grad, (((0,), (0,)), ((), ())), preferred_element_type=jnp.float32
    )
    head_grad = lax.all_to_all(grad_block, DP, split_axis=0, concat_axis=1, tiled=True)
    return (head_grad, scores)


def solution(mesh):
    fine = Mesh(mesh.devices.reshape(2, 4, 2, 16, 2), DP + VOCAB)
    return jax.shard_map(
        local,
        mesh=fine,
        in_specs=(P(DP, None), P(DP), P(DP, None), P(DP), P(), P(DP, VOCAB), P(VOCAB)),
        out_specs=(P(DP, VOCAB), P()),
        check_vma=False,
    )
```

profile of v0, /device:TPU:1, one launch (start us, length us, event | category | flops | bytes accessed | tf_op | source)
XLA Modules:
  0.0 185.7 jit_solution(16136462028311963725)
XLA Ops:
  7.2 0.7 all-gather.2.cloned.1.call-update
  7.9 0.7 copy.29
  8.6 0.7 copy.28
  9.4 0.8 pad_add_fusion
  10.1 0.6 broadcast_in_dim.12
  10.7 10.1 %all-to-all-start = ((s32[16,2,18]{2,1,0:T(2,128)}), s32[16,2,18]{2,1,0:T(2,128)S(1)}, u32[]{:S(2)}, u32[]{:S(2)}) async-start(s32[16,2,18]{2,1,0:T(2,128)} %broadcast_in_dim.12), calls=%async_computation | async-start | bytes 32768 | tf_op jit(solution)/shard_map/all_to_all | solution.py:22
  20.9 2.3 %copy.30 = bf16[128,4096]{0,1:T(8,128)(2,1)} copy(bf16[128,4096]{1,0:T(8,128)(2,1)} %param.12) | data formatting | bytes 2097152 | tf_op args[5]
  23.1 3.6 %all-to-all-done = s32[16,2,18]{2,1,0:T(2,128)S(1)} async-done(((s32[16,2,18]{2,1,0:T(2,128)}), s32[16,2,18]{2,1,0:T(2,128)S(1)}, u32[]{:S(2)}, u32[]{:S(2)}) %all-to-all-start) | async-done | bytes 2336 | tf_op jit(solution)/shard_map/all_to_all | solution.py:22
  26.7 3.8 %all-to-all-start.1 = ((bf16[128,16,256]{0,2,1:T(8,128)(2,1)}), bf16[128,16,256]{0,2,1:T(8,128)(2,1)S(1)}, u32[]{:S(2)}, u32[]{:S(2)}) async-start(bf16[128,16,256]{0,2,1:T(8,128)(2,1)} %bitcast.3), calls=%async_computation.1 | async-start | bytes 2097152 | tf_op jit(solution)/shard_map/all_to_all | solution.py:39
  31.2 0.3 convert_reduce_fusion
  31.4 24.5 %all-to-all-done.1 = bf16[128,16,256]{0,2,1:T(8,128)(2,1)S(1)} async-done(((bf16[128,16,256]{0,2,1:T(8,128)(2,1)}), bf16[128,16,256]{0,2,1:T(8,128)(2,1)S(1)}, u32[]{:S(2)}, u32[]{:S(2)}) %all-to-all-start.1) | async-done | bytes 1048608 | tf_op jit(solution)/shard_map/all_to_all | solution.py:39
  55.9 0.5 copy.31
  56.5 29.3 %all-gather.2.cloned.1.call-done = bf16[2048,2048]{1,0:T(8,128)(2,1)} async-done(((bf16[128,2048]{1,0:T(8,128)(2,1)}), bf16[2048,2048]{1,0:T(8,128)(2,1)}) %all-gather.2.cloned.1.call-update) | async-done | bytes 8388624 | tf_op jit(solution)/shard_map/all_gather | solution.py:40
  85.7 7.4 %multiply_reduce_fusion = (f32[256]{0:T(256)S(1)}, f32[2048,256]{1,0:T(8,128)S(1)}) fusion(f32[2048]{0:T(1024)S(1)} %div.40, bf16[2048,2048]{1,0:T(8,128)(2,1)} %all-gather.2.cloned.1.call-done, bf16[2048,256]{1,0:T(8,128)(2,1)S(1)} %bitcast.34), kind=kOutput, calls=%fused_computation.5 | convolution fusion | flops 2151677696 | bytes 11543552 | tf_op jit(solution)/shard_map/dot_general | solution.py:43
  93.1 1.9 %multiply_reduce_fusion.1 = f32[32,256]{1,0:T(8,128)S(1)} fusion(f32[32,64]{1,0:T(8,128)S(1)} %convert_divide_fusion, f32[2048,256]{1,0:T(8,128)S(1)} %get-tuple-element.9), kind=kLoop, calls=%fused_computation.6 | loop fusion | flops 4186112 | bytes 2138112 | tf_op jit(solution)/shard_map/reduce_sum | solution.py:50
  95.3 0.9 reshape.108
  96.2 5.2 %all-to-all-start.2 = ((f32[32,1,1024]{2,1,0:T(1,128)}), f32[32,1,1024]{2,1,0:T(1,128)S(1)}, u32[]{:S(2)}, u32[]{:S(2)}) async-start(f32[32,1,1024]{2,1,0:T(1,128)} %reshape.108), calls=%async_computation.2 | async-start | bytes 262144 | tf_op jit(solution)/shard_map/all_to_all | solution.py:22
  101.4 7.7 %all-to-all-done.2 = f32[32,1,1024]{2,1,0:T(1,128)S(1)} async-done(((f32[32,1,1024]{2,1,0:T(1,128)}), f32[32,1,1024]{2,1,0:T(1,128)S(1)}, u32[]{:S(2)}, u32[]{:S(2)}) %all-to-all-start.2) | async-done | bytes 131104 | tf_op jit(solution)/shard_map/all_to_all | solution.py:22
  109.1 0.5 broadcast.88
  109.6 0.9 reduce.8
  110.8 0.8 reshape.110
  111.6 13.1 %all-to-all-start.3 = ((f32[16,1,1024]{2,1,0:T(1,128)}), f32[16,1,1024]{2,1,0:T(1,128)S(1)}, u32[]{:S(2)}, u32[]{:S(2)}) async-start(f32[16,1,1024]{2,1,0:T(1,128)} %reshape.110), calls=%async_computation.3 | async-start | bytes 131072 | tf_op jit(solution)/shard_map/all_to_all | solution.py:22
  124.8 0.8 multiply_multiply_fusion
  125.5 10.8 %all-to-all-done.3 = f32[16,1,1024]{2,1,0:T(1,128)S(1)} async-done(((f32[16,1,1024]{2,1,0:T(1,128)}), f32[16,1,1024]{2,1,0:T(1,128)S(1)}, u32[]{:S(2)}, u32[]{:S(2)}) %all-to-all-start.3) | async-done | bytes 65568 | tf_op jit(solution)/shard_map/all_to_all | solution.py:22
  136.3 0.8 reduce.9
  137.5 0.2 fusion.12
  137.6 0.3 convolution_add_fusion
  138.0 1.7 fusion.1
  139.7 5.7 %convolution_bitcast_fusion = f32[32,16,8,128]{3,2,1,0:T(8,128)S(1)} fusion(bf16[2048,256]{1,0:T(8,128)(2,1)S(1)} %fusion.1, bf16[2048,2048]{1,0:T(8,128)(2,1)} %all-gather.2.cloned.1.call-done), kind=kOutput, calls=%fused_computation.8 | convolution fusion | flops 2147483648 | bytes 11534336 | tf_op jit(solution)/shard_map/dot_general | solution.py:83
  145.5 0.2 copy.36
  145.7 31.3 %all_to_all.53 = f32[16,128,256]{1,2,0:T(8,128)S(1)} all-to-all(f32[16,128,256]{1,2,0:T(8,128)S(1)} %bitcast.31), channel_id=1, replica_groups=mesh['xl'=2,'y'=4,'c'=2,'z'=16,'xh'=2] {'xl','y','c'}, dimensions={0} | all-to-all | bytes 4194304 | tf_op jit(solution)/shard_map/all_to_all | solution.py:86
  177.0 1.8 copy.33
  (20 shorter events, 1.4 us)
Async XLA Ops:
  7.2 78.6 %all-gather.2.cloned.1.call-start = ((), (), s32[]{:S(2)}) async-start(), calls=%async_computation.5 | async-start | bytes 8912896 | tf_op jit(solution)/shard_map/all_gather | solution.py:40
  10.7 16.0 %all-to-all-start = ((s32[16,2,18]{2,1,0:T(2,128)}), s32[16,2,18]{2,1,0:T(2,128)S(1)}, u32[]{:S(2)}, u32[]{:S(2)}) async-start(s32[16,2,18]{2,1,0:T(2,128)} %broadcast_in_dim.12), calls=%async_computation | async-start | bytes 32768 | tf_op jit(solution)/shard_map/all_to_all | solution.py:22
  26.7 29.2 %all-to-all-start.1 = ((bf16[128,16,256]{0,2,1:T(8,128)(2,1)}), bf16[128,16,256]{0,2,1:T(8,128)(2,1)S(1)}, u32[]{:S(2)}, u32[]{:S(2)}) async-start(bf16[128,16,256]{0,2,1:T(8,128)(2,1)} %bitcast.3), calls=%async_computation.1 | async-start | bytes 2097152 | tf_op jit(solution)/shard_map/all_to_all | solution.py:39
  95.2 42.0 %copy-start.1 = (s32[32]{0:T(128)S(1)}, s32[32]{0:T(128)}, u32[]{:S(2)}) copy-start(s32[32]{0:T(128)} %param.11) | copy-start | bytes 388
  96.2 12.9 %all-to-all-start.2 = ((f32[32,1,1024]{2,1,0:T(1,128)}), f32[32,1,1024]{2,1,0:T(1,128)S(1)}, u32[]{:S(2)}, u32[]{:S(2)}) async-start(f32[32,1,1024]{2,1,0:T(1,128)} %reshape.108), calls=%async_computation.2 | async-start | bytes 262144 | tf_op jit(solution)/shard_map/all_to_all | solution.py:22
  111.6 24.7 %all-to-all-start.3 = ((f32[16,1,1024]{2,1,0:T(1,128)}), f32[16,1,1024]{2,1,0:T(1,128)S(1)}, u32[]{:S(2)}, u32[]{:S(2)}) async-start(f32[16,1,1024]{2,1,0:T(1,128)} %reshape.110), calls=%async_computation.3 | async-start | bytes 131072 | tf_op jit(solution)/shard_map/all_to_all | solution.py:22
  137.3 8.2 %copy-start = (f32[32,32]{1,0:T(8,128)}, f32[32,32]{1,0:T(8,128)S(1)}, u32[]{:S(2)}) copy-start(f32[32,32]{1,0:T(8,128)S(1)} %reduce_sum.75) | copy-start | bytes 12292
Sparse Core Ops, SparseCore 0:
  10.1 75.5 all-gather.1
where the time goes:
time: 186 us
  waiting for transfers between devices  76.5 us (41%)
  starting transfers between devices  32.3 us (17%)
  blocking collectives  31.3 us (17%)
  between operations  14.2 us (8%)
  matrix products  13.6 us (7%)
  local copies, waits for them, and re-layouts  9.72 us (5%)
  other arithmetic  8.02 us (4%)
    all_to_all x1, blocking collectives, local(): lax.all_to_all(grad_block, DP, split_axis=0, concat_axis=1, tiled=True)  31.3 us
    all_gather x1, waiting for transfers between devices, local(): hidden_all = lax.all_gather(passage_hidden, DP, axis=0, tiled=True)  29.3 us
    all_to_all x3, starting transfers between devices, spread(): lax.all_to_all(jnp.broadcast_to(value[None], (count,) + value.shape), axe...  28.4 us
    all_to_all x1, waiting for transfers between devices, local(): lax.all_to_all(head, DP, split_axis=1, concat_axis=0, tiled=True)  24.5 us
    all_to_all x3, waiting for transfers between devices, spread(): lax.all_to_all(jnp.broadcast_to(value[None], (count,) + value.shape), axe...  22 us
    dot_general x1, matrix products, local(): logits = jnp.dot(hidden_all, head_block, preferred_element_type=jnp.float32)  7.39 us
    unnamed x10, local copies, waits for them, and re-layouts  6.06 us
    dot_general x1, matrix products, local(): lax.dot_general(hidden_all, logit_grad, (((0,), (0,)), ((), ())), preferr...  5.74 us
  transfers between devices with their start and end apart: 5, of which 5 were waited for; matrix products, arithmetic and copies ran while one was open for 4% of the time, Pallas kernels for 0%

commit v1 on v0

--- a/solution.py
+++ b/solution.py
@@ -37,7 +37,9 @@
     query_sizes = packed[:, query_slots]
     passage_sizes = packed[:, query_slots + 1]
     head_block = lax.all_to_all(head, DP, split_axis=1, concat_axis=0, tiled=True)
-    hidden_all = lax.all_gather(passage_hidden, DP, axis=0, tiled=True)
+    hidden_all = jnp.concatenate(
+        lax.all_to_all(jnp.stack([passage_hidden] * lax.axis_size(DP)), DP, 0, 0), axis=0
+    )
     passage_count = passage_sizes.shape[0]
     seq_span = hidden_all.shape[0] // passage_count
     logits = jnp.dot(hidden_all, head_block, preferred_element_type=jnp.float32)

time: 186 us -> 269 us (1.45)
  waiting for transfers between devices: 76.5 us -> 142 us
  blocking collectives: 31.3 us -> 49.5 us
  between operations: 14.2 us -> 0.82 us
  starting transfers between devices: 32.3 us -> 40.8 us
  local copies, waits for them, and re-layouts: 9.72 us -> 13.4 us
    all_to_all x1, waiting for transfers between devices: 24.5 us -> 120 us  [local(): lax.all_to_all(jnp.stack([passage_hidden] * lax.axis_size(DP)), DP, 0, 0)]
    all_gather x1 -> x0, waiting for transfers between devices: 29.3 us -> none  [local(): hidden_all = lax.all_gather(passage_hidden, DP, axis=0, tiled=True)]
    all_to_all x0 -> x1, blocking collectives: none -> 18.2 us  [local(): lax.all_to_all(head, DP, split_axis=1, concat_axis=0, tiled=True)]
    all_to_all x3, starting transfers between devices: 28.4 us -> 35.1 us  [spread(): lax.all_to_all(jnp.broadcast_to(value[None], (count,) + value.shape), axe...]
    another operation x0 -> x1, local copies, waits for them, and re-layouts: none -> 4.3 us  [local(): jnp.stack([passage_hidden] * lax.axis_size(DP))]
    unnamed x10 -> x12, local copies, waits for them, and re-layouts: 6.06 us -> 5.48 us
  transfers between devices with their start and end apart: 5 -> 4, of which waited for: 5 -> 4; matrix products, arithmetic and copies ran while one was open for 4% -> 1% of each run, Pallas kernels for 0% -> 0%
where the time goes in v1:
time: 269 us
  waiting for transfers between devices  142 us (53%)
  blocking collectives  49.5 us (18%)
  starting transfers between devices  40.8 us (15%)
  matrix products  13.6 us (5%)
  local copies, waits for them, and re-layouts  13.4 us (5%)
  other arithmetic  8.02 us (3%)
    all_to_all x1, waiting for transfers between devices, local(): lax.all_to_all(jnp.stack([passage_hidden] * lax.axis_size(DP)), DP, 0, 0)  120 us
    all_to_all x3, starting transfers between devices, spread(): lax.all_to_all(jnp.broadcast_to(value[None], (count,) + value.shape), axe...  35.1 us
    all_to_all x1, blocking collectives, local(): lax.all_to_all(grad_block, DP, split_axis=0, concat_axis=1, tiled=True)  31.3 us
    all_to_all x3, waiting for transfers between devices, spread(): lax.all_to_all(jnp.broadcast_to(value[None], (count,) + value.shape), axe...  22.6 us
    all_to_all x1, blocking collectives, local(): lax.all_to_all(head, DP, split_axis=1, concat_axis=0, tiled=True)  18.2 us
    dot_general x1, matrix products, local(): logits = jnp.dot(hidden_all, head_block, preferred_element_type=jnp.float32)  7.38 us
    dot_general x1, matrix products, local(): lax.dot_general(hidden_all, logit_grad, (((0,), (0,)), ((), ())), preferr...  5.74 us
    all_to_all x1, starting transfers between devices, local(): lax.all_to_all(jnp.stack([passage_hidden] * lax.axis_size(DP)), DP, 0, 0)  5.72 us
  transfers between devices with their start and end apart: 4, of which 4 were waited for; matrix products, arithmetic and copies ran while one was open for 1% of the time, Pallas kernels for 0%

profile of v1, /device:TPU:1, one launch (start us, length us, event | category | flops | bytes accessed | tf_op | source)
XLA Modules:
  0.0 268.7 jit_solution(3497109382755291323)
XLA Ops:
  0.6 0.7 copy.29
  1.4 0.7 copy.28
  2.1 0.8 pad_add_fusion
  2.9 0.6 broadcast_in_dim.12
  3.5 10.1 %all-to-all-start = ((s32[16,2,18]{2,1,0:T(2,128)}), s32[16,2,18]{2,1,0:T(2,128)S(1)}, u32[]{:S(2)}, u32[]{:S(2)}) async-start(s32[16,2,18]{2,1,0:T(2,128)} %broadcast_in_dim.12), calls=%async_computation | async-start | bytes 32768 | tf_op jit(solution)/shard_map/all_to_all | solution.py:22
  13.6 1.7 copy.30
  15.3 4.2 %all-to-all-done = s32[16,2,18]{2,1,0:T(2,128)S(1)} async-done(((s32[16,2,18]{2,1,0:T(2,128)}), s32[16,2,18]{2,1,0:T(2,128)S(1)}, u32[]{:S(2)}, u32[]{:S(2)}) %all-to-all-start) | async-done | bytes 2336 | tf_op jit(solution)/shard_map/all_to_all | solution.py:22
  19.5 18.2 %all_to_all.58 = bf16[128,16,256]{0,2,1:T(8,128)(2,1)S(1)} all-to-all(bf16[128,16,256]{0,2,1:T(8,128)(2,1)S(1)} %bitcast.35), channel_id=1, replica_groups=mesh['xl'=2,'y'=4,'c'=2,'z'=16,'xh'=2] {'xl','y','c'}, dimensions={1} | all-to-all | bytes 2097152 | tf_op jit(solution)/shard_map/all_to_all | solution.py:39
  37.7 4.3 %stack.2 = bf16[16,128,2048]{2,1,0:T(8,128)(2,1)} broadcast(bf16[128,2048]{1,0:T(8,128)(2,1)S(1)} %copy-done), dimensions={1,2} | broadcast | bytes 8912896 | tf_op jit(solution)/shard_map/stack | solution.py:41
  42.0 5.7 %all-to-all-start.1 = ((bf16[16,128,2048]{2,1,0:T(8,128)(2,1)}), bf16[16,128,2048]{2,1,0:T(8,128)(2,1)}, u32[]{:S(2)}, u32[]{:S(2)}) async-start(bf16[16,128,2048]{2,1,0:T(8,128)(2,1)} %stack.2), calls=%async_computation.1 | async-start | bytes 16777216 | tf_op jit(solution)/shard_map/all_to_all | solution.py:41
  48.3 0.3 convert_reduce_fusion
  48.6 0.5 copy.31
  49.1 119.9 %all-to-all-done.1 = bf16[16,128,2048]{2,1,0:T(8,128)(2,1)} async-done(((bf16[16,128,2048]{2,1,0:T(8,128)(2,1)}), bf16[16,128,2048]{2,1,0:T(8,128)(2,1)}, u32[]{:S(2)}, u32[]{:S(2)}) %all-to-all-start.1) | async-done | bytes 8388640 | tf_op jit(solution)/shard_map/all_to_all | solution.py:41
  169.0 7.4 %multiply_reduce_fusion = (f32[256]{0:T(256)S(1)}, f32[2048,256]{1,0:T(8,128)S(1)}) fusion(f32[2048]{0:T(1024)S(1)} %div.40, bf16[2048,2048]{1,0:T(8,128)(2,1)} %bitcast.3, bf16[2048,256]{1,0:T(8,128)(2,1)S(1)} %bitcast.36), kind=kOutput, calls=%fused_computation.5 | convolution fusion | flops 2151677696 | bytes 11543552 | tf_op jit(solution)/shard_map/dot_general | solution.py:45
  176.3 1.9 multiply_reduce_fusion.1
  178.5 0.9 reshape.114
  179.4 11.9 %all-to-all-start.3 = ((f32[32,1,1024]{2,1,0:T(1,128)}), f32[32,1,1024]{2,1,0:T(1,128)S(1)}, u32[]{:S(2)}, u32[]{:S(2)}) async-start(f32[32,1,1024]{2,1,0:T(1,128)} %reshape.114), calls=%async_computation.3 | async-start | bytes 262144 | tf_op jit(solution)/shard_map/all_to_all | solution.py:22
  191.4 7.7 %all-to-all-done.3 = f32[32,1,1024]{2,1,0:T(1,128)S(1)} async-done(((f32[32,1,1024]{2,1,0:T(1,128)}), f32[32,1,1024]{2,1,0:T(1,128)S(1)}, u32[]{:S(2)}, u32[]{:S(2)}) %all-to-all-start.3) | async-done | bytes 131104 | tf_op jit(solution)/shard_map/all_to_all | solution.py:22
  199.0 0.5 broadcast.90
  199.5 0.9 reduce.8
  200.8 0.8 reshape.116
  201.6 13.0 %all-to-all-start.4 = ((f32[16,1,1024]{2,1,0:T(1,128)}), f32[16,1,1024]{2,1,0:T(1,128)S(1)}, u32[]{:S(2)}, u32[]{:S(2)}) async-start(f32[16,1,1024]{2,1,0:T(1,128)} %reshape.116), calls=%async_computation.4 | async-start | bytes 131072 | tf_op jit(solution)/shard_map/all_to_all | solution.py:22
  214.6 0.8 multiply_multiply_fusion
  215.4 10.8 %all-to-all-done.4 = f32[16,1,1024]{2,1,0:T(1,128)S(1)} async-done(((f32[16,1,1024]{2,1,0:T(1,128)}), f32[16,1,1024]{2,1,0:T(1,128)S(1)}, u32[]{:S(2)}, u32[]{:S(2)}) %all-to-all-start.4) | async-done | bytes 65568 | tf_op jit(solution)/shard_map/all_to_all | solution.py:22
  226.2 0.8 reduce.9
  227.3 0.2 fusion.12
  227.5 0.3 convolution_add_fusion
  227.8 1.7 fusion.1
  229.6 5.7 %convolution_bitcast_fusion = f32[32,16,8,128]{3,2,1,0:T(8,128)S(1)} fusion(bf16[2048,256]{1,0:T(8,128)(2,1)S(1)} %fusion.1, bf16[2048,2048]{1,0:T(8,128)(2,1)} %bitcast.3), kind=kOutput, calls=%fused_computation.8 | convolution fusion | flops 2147483648 | bytes 11534336 | tf_op jit(solution)/shard_map/dot_general | solution.py:85
  235.3 0.2 copy.36
  235.5 31.3 %all_to_all.59 = f32[16,128,256]{1,2,0:T(8,128)S(1)} all-to-all(f32[16,128,256]{1,2,0:T(8,128)S(1)} %bitcast.32), channel_id=1, replica_groups=mesh['xl'=2,'y'=4,'c'=2,'z'=16,'xh'=2] {'xl','y','c'}, dimensions={0} | all-to-all | bytes 4194304 | tf_op jit(solution)/shard_map/all_to_all | solution.py:88
  266.9 1.8 copy.33
  (21 shorter events, 1.4 us)
Async XLA Ops:
  3.5 16.0 %all-to-all-start = ((s32[16,2,18]{2,1,0:T(2,128)}), s32[16,2,18]{2,1,0:T(2,128)S(1)}, u32[]{:S(2)}, u32[]{:S(2)}) async-start(s32[16,2,18]{2,1,0:T(2,128)} %broadcast_in_dim.12), calls=%async_computation | async-start | bytes 32768 | tf_op jit(solution)/shard_map/all_to_all | solution.py:22
  13.6 24.1 %copy-start = (bf16[128,2048]{1,0:T(8,128)(2,1)S(1)}, bf16[128,2048]{1,0:T(8,128)(2,1)}, u32[]{:S(2)}) copy-start(bf16[128,2048]{1,0:T(8,128)(2,1)} %param.7) | copy-start | bytes 1572868
  42.0 127.0 %all-to-all-start.1 = ((bf16[16,128,2048]{2,1,0:T(8,128)(2,1)}), bf16[16,128,2048]{2,1,0:T(8,128)(2,1)}, u32[]{:S(2)}, u32[]{:S(2)}) async-start(bf16[16,128,2048]{2,1,0:T(8,128)(2,1)} %stack.2), calls=%async_computation.1 | async-start | bytes 16777216 | tf_op jit(solution)/shard_map/all_to_all | solution.py:41
  178.4 48.7 %copy-start.2 = (s32[32]{0:T(128)S(1)}, s32[32]{0:T(128)}, u32[]{:S(2)}) copy-start(s32[32]{0:T(128)} %param.11) | copy-start | bytes 388
  179.4 19.6 %all-to-all-start.3 = ((f32[32,1,1024]{2,1,0:T(1,128)}), f32[32,1,1024]{2,1,0:T(1,128)S(1)}, u32[]{:S(2)}, u32[]{:S(2)}) async-start(f32[32,1,1024]{2,1,0:T(1,128)} %reshape.114), calls=%async_computation.3 | async-start | bytes 262144 | tf_op jit(solution)/shard_map/all_to_all | solution.py:22
  201.6 24.6 %all-to-all-start.4 = ((f32[16,1,1024]{2,1,0:T(1,128)}), f32[16,1,1024]{2,1,0:T(1,128)S(1)}, u32[]{:S(2)}, u32[]{:S(2)}) async-start(f32[16,1,1024]{2,1,0:T(1,128)} %reshape.116), calls=%async_computation.4 | async-start | bytes 131072 | tf_op jit(solution)/shard_map/all_to_all | solution.py:22
  227.1 8.2 %copy-start.1 = (f32[32,32]{1,0:T(8,128)}, f32[32,32]{1,0:T(8,128)S(1)}, u32[]{:S(2)}) copy-start(f32[32,32]{1,0:T(8,128)S(1)} %reduce_sum.75) | copy-start | bytes 12292
